TPU v7x, 1024 devices: a whole 4x8x16 slice. The times are simulated.
1024 devices in a mesh: ctx: 64 (over z, x), tp: 16 (over y, core).
Axes of the slice: x: 4, y: 8, z: 16, core: 2. Of those that a mesh axis runs over, the one named last changes fastest.
Arguments:
- gate_q: bfloat16 [4096, 16384], P('tp', 'ctx'), may hold values from -6 to 6
- key_k: bfloat16 [4096, 16384], P('tp', 'ctx'), may hold values from -6 to 6
- value_v: bfloat16 [4096, 16384], P('tp', 'ctx'), may hold values from -6 to 6
- filter_taps: float32 [4096, 16384], P('tp', 'ctx'), may hold values from -1 to 1
- skip_bias: float32 [4096], P('tp'), may hold values from 0.5 to 1.5
- w_out: bfloat16 [4096, 4096], P('tp'), may hold values from -0.125 to 0.125
Outputs:
- mixed: bfloat16 [4096, 16384], P('tp', 'ctx')
All inputs are finite; a program needn't handle non-finite values.
Results may differ from a plain program's by a relative error of at most 0.018.
Values may be sent and summed in bfloat16 or wider, within the bound.
A program may use at most 32 MiB of HBM per device.

v0:
```python
import math

import jax
import jax.numpy as jnp
import numpy as np
from jax import lax
from jax.sharding import PartitionSpec as P

TOP = lax.Precision.HIGHEST
R = 128


def tables():
    length = R * R
    row = np.arange(R)
    shifted = row - 0.25
    first = 2.0 * np.pi * np.outer(shifted, row) / R
    twist = 2.0 * np.pi * np.outer(shifted, row) / length
    second = 2.0 * np.pi * np.outer(row, row) / R
    forward_a = np.stack([np.cos(first), -np.sin(first)])
    forward_b = np.block(
        [[np.cos(second), -np.sin(second)], [np.sin(second), np.cos(second)]]
    )
    back_b = forward_b.T
    back_a = np.stack([np.cos(first).T, -np.sin(first).T]) / length
    as32 = lambda t: np.asarray(t, np.float32)
    return tuple(map(as32, (forward_a, np.cos(twist), np.sin(twist), forward_b, back_b, back_a)))


def convolve(pair):
    forward_a, cos_t, sin_t, forward_b, back_b, back_a = tables()
    grid = pair.astype(jnp.float32).reshape(2, pair.shape[1], R, R)
    mid = jnp.einsum("rka,scab->rsckb", forward_a, grid, precision=TOP)
    re, im = mid[0], mid[1]
    mid = jnp.concatenate([re * cos_t + im * sin_t, im * cos_t - re * sin_t], axis=-1)
    spec = jnp.einsum("sckb,bm->sckm", mid, forward_b, precision=TOP)
    re, im = spec[..., :R], spec[..., R:]
    prod = jnp.concatenate([re[0] * re[1] - im[0] * im[1], re[0] * im[1] + im[0] * re[1]], axis=-1)
    mid = jnp.einsum("ckm,mb->ckb", prod, back_b, precision=TOP)
    re, im = mid[..., :R], mid[..., R:]
    re, im = re * cos_t - im * sin_t, im * cos_t + re * sin_t
    out = jnp.einsum("ak,ckb->cab", back_a[0], re, precision=TOP)
    out = out + jnp.einsum("ak,ckb->cab", back_a[1], im, precision=TOP)
    return out.reshape(out.shape[0], R * R)


def body(gate_q, key_k, value_v, filter_taps, skip_bias, w_out):
    signal = key_k.astype(jnp.float32) * value_v.astype(jnp.float32)
    pair = jnp.stack([signal.astype(jnp.bfloat16), filter_taps.astype(jnp.bfloat16)])
    pair = lax.all_to_all(pair, "ctx", split_axis=1, concat_axis=2, tiled=True)
    values = convolve(pair).astype(jnp.bfloat16)
    convolved = lax.all_to_all(values, "ctx", split_axis=1, concat_axis=0, tiled=True)
    gated_vals = (
        gate_q.astype(jnp.float32)
        * (convolved.astype(jnp.float32) + skip_bias[:, None] * signal)
    ).astype(jnp.bfloat16)
    return lax.psum_scatter(
        lax.dot_general(
            w_out, gated_vals, (((0,), (0,)), ((), ())), preferred_element_type=jnp.float32
        ).astype(jnp.bfloat16),
        "tp",
        scatter_dimension=0,
        tiled=True,
    )


def solution(mesh):
    return jax.shard_map(
        body,
        mesh=mesh,
        in_specs=(
            P("tp", "ctx"),
            P("tp", "ctx"),
            P("tp", "ctx"),
            P("tp", "ctx"),
            P("tp"),
            P("tp", None),
        ),
        out_specs=P("tp", "ctx"),
        check_vma=False,
    )
```

profile of v0, /device:TPU:1, one launch (start us, length us, event | category | flops | bytes accessed | tf_op | source)
XLA Modules:
  0.0 147.5 jit_solution(17127925627826561302)
XLA Ops:
  6.5 0.0 copy-start
  6.5 0.0 copy-start.8
  6.5 0.0 reduce-scatter.2.cloned.1.call-start
  6.5 1.3 fusion.24
  7.8 0.0 copy-start.9
  7.8 0.0 copy-start.10
  7.9 0.3 copy.42
  8.2 41.8 %all_to_all.25 = bf16[2,256,256]{2,0,1:T(2,128)(2,1)S(1)} all-to-all(bf16[2,256,256]{2,0,1:T(2,128)(2,1)S(1)} %copy.42), channel_id=1, replica_groups=mesh['ctx'=64,'tp'=16] {'ctx'}, dimensions={1} | all-to-all | bytes 524288 | tf_op jit(solution)/shard_map/all_to_all | solution.py:50
  50.0 0.0 copy-start.4
  50.0 0.1 reshape.23
  50.1 0.0 copy-done.8
  50.1 0.6 convolution_bitcast_fusion
  50.8 0.0 copy-done.9
  50.8 0.0 copy-done.10
  50.8 0.1 multiply_add_fusion
  50.9 0.0 copy-start.3
  50.9 0.0 copy-done.4
  51.0 0.0 copy-start.5
  51.0 0.0 copy-start.6
  51.0 0.0 copy-start.12
  51.0 1.8 %fusion.3 = f32[2,4,128,256]{3,2,1,0:T(8,128)S(1)} fusion(f32[256,256,1,1]{1,0,3,2:T(8,128)S(1)} %copy-done.4, f32[2,4,128,128]{2,3,1,0:T(8,128)S(1)} %get-tuple-element.6, f32[2,4,128,128]{2,3,1,0:T(8,128)S(1)} %get-tuple-element.5), kind=kOutput, calls=%fused_computation.6 | convolution fusion | flops 805568512 | bytes 2359296 | tf_op jit(solution)/shard_map/sckb,bm->sckm/dot_general | solution.py:36
  52.8 0.0 copy-start.11
  52.8 0.1 subtract_bitcast_fusion
  52.9 0.0 copy-done.3
  52.9 0.6 fusion.7
  53.5 0.0 copy-done.5
  53.5 0.0 copy-done.6
  53.5 0.0 copy-done.12
  53.5 0.0 copy-start.1
  53.5 0.0 copy-start.2
  53.5 0.0 copy-start.7
  53.5 0.0 copy-start.13
  53.6 0.6 fusion.15
  54.2 0.0 copy-done.11
  54.2 0.6 fusion.2
  54.8 0.1 copy.51
  55.0 0.1 copy.52
  55.1 22.2 %all_to_all.26 = bf16[4,64,256]{2,0,1:T(4,128)(2,1)S(1)} all-to-all(bf16[4,64,256]{2,0,1:T(4,128)(2,1)S(1)} %copy.52), channel_id=1, replica_groups=mesh['ctx'=64,'tp'=16] {'ctx'}, dimensions={1} | all-to-all | bytes 262144 | tf_op jit(solution)/shard_map/all_to_all | solution.py:52
  77.3 0.1 reshape.24
  77.4 0.0 copy-done
  77.4 0.0 copy-done.1
  77.4 0.0 copy-done.2
  77.4 0.0 copy-done.7
  77.5 0.0 copy-done.13
  77.5 2.2 %fusion = bf16[4096,256]{0,1:T(8,128)(2,1)} fusion(bf16[256,4096]{1,0:T(8,128)(2,1)S(1)} %copy-done, f32[256,256]{1,0:T(8,128)S(1)} %reshape.24, bf16[256,256]{1,0:T(8,128)(2,1)S(1)} %copy-done.7, bf16[256,256]{1,0:T(8,128)(2,1)S(1)} %copy-done.1, bf16[256,256]{1,0:T(8,128)(2,1)S(1)} %copy-done.2, f32[256]{0:T(256)S(1)} %copy-done.13), kind=kOutput, calls=%fused_computation.1 | convolution fusion | flops 538443776 | bytes 4850688 | tf_op jit(solution)/shard_map/dot_general | solution.py:58
  79.6 0.0 reduce-scatter.2.cloned.1.call-update
  79.7 59.4 %reduce-scatter.2.cloned.1.call-done = bf16[256,256]{0,1:T(8,128)(2,1)} async-done(((bf16[4096,256]{0,1:T(8,128)(2,1)}), bf16[256,256]{0,1:T(8,128)(2,1)}) %reduce-scatter.2.cloned.1.call-update) | async-done | bytes 131088 | tf_op jit(solution)/shard_map/reduce_scatter | solution.py:57
  139.0 1.7 %copy.53 = bf16[256,256]{1,0:T(8,128)(2,1)} copy(bf16[256,256]{0,1:T(8,128)(2,1)} %reduce-scatter.2.cloned.1.call-done) | data formatting | bytes 262144 | tf_op jit(solution)/shard_map/reduce_scatter | solution.py:57
  (4 shorter events, 0.1 us)
Async XLA Ops:
  6.5 70.9 %copy-start = (bf16[256,4096]{1,0:T(8,128)(2,1)S(1)}, bf16[256,4096]{1,0:T(8,128)(2,1)}, u32[]{:S(2)}) copy-start(bf16[256,4096]{1,0:T(8,128)(2,1)} %param.18) | copy-start | bytes 6291460
  6.5 43.6 %copy-start.8 = (f32[2,128,128,1,1]{2,1,0,4,3:T(8,128)S(1)}, f32[2,128,128,1,1]{2,1,0,4,3:T(8,128)}, u32[]{:S(2)}) copy-start(f32[2,128,128,1,1]{2,1,0,4,3:T(8,128)} %constant.21) | copy-start | bytes 393220
  6.5 132.5 %reduce-scatter.2.cloned.1.call-start = ((), (), s32[]{:S(2)}) async-start(), calls=%async_computation.3 | async-start | bytes 2228224 | tf_op jit(solution)/shard_map/reduce_scatter | solution.py:57
  7.8 42.9 %copy-start.9 = (f32[128,128]{0,1:T(8,128)S(1)}, f32[128,128]{0,1:T(8,128)}, u32[]{:S(2)}) copy-start(f32[128,128]{0,1:T(8,128)} %constant.16.clone) | copy-start | bytes 196612
  7.8 42.9 %copy-start.10 = (f32[128,128]{0,1:T(8,128)S(1)}, f32[128,128]{0,1:T(8,128)}, u32[]{:S(2)}) copy-start(f32[128,128]{0,1:T(8,128)} %constant.15.clone) | copy-start | bytes 196612
  50.0 1.0 copy-start.4
  50.9 2.0 %copy-start.3 = (f32[256,256,1]{1,0,2:T(8,128)S(1)}, f32[256,256,1]{1,0,2:T(8,128)}, u32[]{:S(2)}) copy-start(f32[256,256,1]{1,0,2:T(8,128)} %constant.23) | copy-start | bytes 786436
  51.0 2.5 %copy-start.5 = (f32[128,128]{1,0:T(8,128)S(1)}, f32[128,128]{1,0:T(8,128)}, u32[]{:S(2)}) copy-start(f32[128,128]{1,0:T(8,128)} %constant.25) | copy-start | bytes 196612
  51.0 2.5 %copy-start.6 = (f32[128,128]{1,0:T(8,128)S(1)}, f32[128,128]{1,0:T(8,128)}, u32[]{:S(2)}) copy-start(f32[128,128]{1,0:T(8,128)} %constant.24) | copy-start | bytes 196612
  51.0 2.5 %copy-start.12 = (f32[128,128,1]{1,0,2:T(8,128)S(1)}, f32[128,128,1]{1,0,2:T(8,128)}, u32[]{:S(2)}) copy-start(f32[128,128,1]{1,0,2:T(8,128)} %constant.26) | copy-start | bytes 196612
  52.8 1.4 copy-start.11
  53.5 23.9 %copy-start.1 = (bf16[256,256]{1,0:T(8,128)(2,1)S(1)}, bf16[256,256]{1,0:T(8,128)(2,1)}, u32[]{:S(2)}) copy-start(bf16[256,256]{1,0:T(8,128)(2,1)} %param.15) | copy-start | bytes 393220
  53.5 23.9 %copy-start.2 = (bf16[256,256]{1,0:T(8,128)(2,1)S(1)}, bf16[256,256]{1,0:T(8,128)(2,1)}, u32[]{:S(2)}) copy-start(bf16[256,256]{1,0:T(8,128)(2,1)} %param.14) | copy-start | bytes 393220
  53.5 23.9 %copy-start.7 = (bf16[256,256]{1,0:T(8,128)(2,1)S(1)}, bf16[256,256]{1,0:T(8,128)(2,1)}, u32[]{:S(2)}) copy-start(bf16[256,256]{1,0:T(8,128)(2,1)} %param.13) | copy-start | bytes 393220
  53.5 23.9 %copy-start.13 = (f32[256]{0:T(256)S(1)}, f32[256]{0:T(256)}, u32[]{:S(2)}) copy-start(f32[256]{0:T(256)} %param.17) | copy-start | bytes 3076
Sparse Core Ops, SparseCore 0:
  79.8 59.1 reduce-scatter.1
where the time goes:
time: 148 us
  blocking collectives  64 us (43%)
  waiting for transfers between devices  59.4 us (40%)
  between operations  13.7 us (9%)
  matrix products  6.4 us (4%)
  local copies, waits for them, and re-layouts  2.55 us (2%)
  other arithmetic  1.52 us (1%)
    reduce_scatter x1, waiting for transfers between devices, body(): lax.psum_scatter(lax.dot_general(w_out, gated_vals, (((0,), (0,)), ((), (...  59.4 us
    all_to_all x1, blocking collectives, body(): pair = lax.all_to_all(pair, 'ctx', split_axis=1, concat_axis=2, tiled=True)  41.8 us
    all_to_all x1, blocking collectives, body(): lax.all_to_all(values, 'ctx', split_axis=1, concat_axis=0, tiled=True)  22.2 us
  transfers between devices with their start and end apart: 1, of which 1 were waited for; matrix products, arithmetic and copies ran while one was open for 0% of the time, Pallas kernels for 0%

commit v1 on v0

v1 whole, which is shorter than its diff:
```python
import functools

import jax
import jax.numpy as jnp
import ml_dtypes
import numpy as np
from jax import lax
from jax.experimental import pallas as pl
from jax.experimental.pallas import tpu as pltpu
from jax.sharding import PartitionSpec as P

MESH = pl.DeviceIdType.MESH
F32 = jnp.float32
BF16 = jnp.bfloat16
NX = 4


def split_np(table):
    high = np.asarray(table, np.float32).astype(ml_dtypes.bfloat16)
    low = (table - high.astype(np.float64)).astype(ml_dtypes.bfloat16)
    return [high, low]


def tables(nz, nx, own, width):
    shards = nz * nx
    length = shards * width
    freq = np.arange(shards) - 0.25
    block = np.array([z * nx + x for x in range(nx) for z in range(nz)])
    first = 2.0 * np.pi * np.outer(freq, block) / shards
    eye = np.eye(own)
    spread = lambda m: np.einsum("ki,cd->ckid", m, eye).reshape(own * shards, shards * own)
    ahead = np.stack(split_np(spread(np.cos(first))) + split_np(spread(-np.sin(first))))
    back = np.stack(
        split_np(spread(np.cos(first)).T / length) + split_np(spread(-np.sin(first)).T / length)
    )
    angle = 2.0 * np.pi * np.outer(freq, np.arange(width)) / length
    twist = np.stack([np.cos(angle), np.sin(angle)]).astype(np.float32)
    angle = 2.0 * np.pi * (np.outer(np.arange(width), np.arange(width)) % width) / width
    inner = np.stack(split_np(np.cos(angle)) + split_np(np.sin(angle)))
    rows = shards * own
    order = np.arange(rows).reshape(nz, nx, own).transpose(1, 0, 2).reshape(-1)
    to_x = np.zeros((rows, rows))
    to_x[np.arange(rows), order] = 1.0
    perm = np.stack([to_x, to_x.T]).astype(ml_dtypes.bfloat16)
    return ahead, back, twist, inner, perm


def dot(a, b):
    return jnp.dot(a, b, preferred_element_type=F32)


def split(a):
    high = a.astype(BF16)
    return high, (a - high.astype(F32)).astype(BF16)


def dot3(a, b):
    return dot(a[0], b[0]) + (dot(a[0], b[1]) + dot(a[1], b[0]))


def kernel(
    nz, nx, ny,
    gate, key, value, taps, skip, w, ahead, back, twist, inner, perm,
    out,
    sig, skip_cols, w_t, zsend, zbuf, xsend, xbuf, spec, csend, cbuf, dsend, conv,
    psend, precv, own, rsend, rrecv,
    zs_sem, zr_sem, xs_sem, xr_sem, ps_sem, pr_sem, rs_sem, rr_sem,
):
    channels, width = key.shape
    shards = nz * nx
    mine = channels // shards
    zrows = nx * mine
    xrows = nz * mine
    drows = out.shape[0]
    half = width // 2
    ctx = lax.axis_index("ctx")
    tp = lax.axis_index("tp")
    z, x = ctx // nx, ctx % nx
    y, core = tp // 2, tp % 2

    def z_at(o):
        return (z + o + nz) % nz

    def x_at(o):
        return (x + o) % nx

    def y_at(o):
        return (y + o + ny) % ny

    def z_peer(o):
        return {"ctx": z_at(o) * nx + x}

    def x_peer(o):
        return {"ctx": z * nx + x_at(o)}

    def y_peer(o):
        return {"tp": y_at(o) * 2 + core}

    partner = {"tp": y * 2 + (1 - core)}
    z_order = [nz // 2]
    for o in range(nz // 2 - 1, 0, -1):
        z_order += [o, -o]
    x_order = list(range(1, nx))

    barrier = pltpu.get_barrier_semaphore()
    peers = [z_peer(o) for o in z_order] + [x_peer(o) for o in x_order]
    peers += [partner, y_peer(1), y_peer(-1)]
    for peer in peers:
        pl.semaphore_signal(barrier, inc=1, device_id=peer, device_id_type=MESH)

    started = []

    def rows_z(i):
        return pl.ds(pl.multiple_of(i * zrows, zrows), zrows)

    def rows_x(i):
        return pl.ds(pl.multiple_of(i * xrows, xrows), xrows)

    def z_copy(kind, source, target, n, o):
        return pltpu.make_async_remote_copy(
            src_ref=source.at[rows_z(z_at(o))],
            dst_ref=target.at[rows_z(z)],
            send_sem=zs_sem.at[kind, n],
            recv_sem=zr_sem.at[kind, n],
            device_id=z_peer(o),
            device_id_type=MESH,
        )

    def x_copy(kind, source, target, n, o):
        return pltpu.make_async_remote_copy(
            src_ref=source.at[rows_x(x_at(o))],
            dst_ref=target.at[rows_x(x)],
            send_sem=xs_sem.at[kind, n],
            recv_sem=xr_sem.at[kind, n],
            device_id=x_peer(o),
            device_id_type=MESH,
        )

    def z_start(kind, source, target):
        copies = [z_copy(kind, source, target, n, o) for n, o in enumerate(z_order)]
        for copy in copies:
            copy.start()
        target[rows_z(z), :] = source[rows_z(z), :]
        started.extend(copies)
        return copies

    def x_start(kind, source, target):
        copies = [x_copy(kind, source, target, n, o) for n, o in enumerate(x_order)]
        for copy in copies:
            copy.start()
        target[rows_x(x), :] = source[rows_x(x), :]
        started.extend(copies)
        return copies

    def arrive(copies):
        for copy in copies:
            copy.wait_recv()

    tall = lambda t: jnp.concatenate([t] * mine, axis=0)

    def forward(rows):
        re = dot(ahead[0], rows) + dot(ahead[1], rows)
        im = dot(ahead[2], rows) + dot(ahead[3], rows)
        cos_t, sin_t = tall(twist[0]), tall(twist[1])
        mid_re, mid_im = split(re * cos_t + im * sin_t), split(im * cos_t - re * sin_t)
        cos_p, sin_p = (inner[0], inner[1]), (inner[2], inner[3])
        return (
            dot3(mid_re, cos_p) + dot3(mid_im, sin_p),
            dot3(mid_im, cos_p) - dot3(mid_re, sin_p),
        )

    zsend[0] = taps[...].astype(BF16)
    pl.semaphore_wait(barrier, len(peers))
    taps_z = z_start(0, zsend.at[0], zbuf.at[0])
    sig[...] = key[...].astype(F32) * value[...].astype(F32)
    zsend[1] = sig[...].astype(BF16)
    sig_z = z_start(1, zsend.at[1], zbuf.at[1])

    skip_cols[...] = jnp.broadcast_to(skip[...], (width, channels)).T
    for j in range(w.shape[1] // drows):
        w_t[pl.ds(j * drows, drows), :] = w[:, pl.ds(j * drows, drows)].T

    arrive(taps_z)
    xsend[0] = dot(perm[0], zbuf[0]).astype(BF16)
    taps_x = x_start(0, xsend.at[0], xbuf.at[0])
    arrive(taps_x)
    spec_re, spec_im = forward(xbuf[0])
    spec[0] = spec_re
    spec[1] = spec_im
    arrive(sig_z)
    xsend[1] = dot(perm[0], zbuf[1]).astype(BF16)
    sig_x = x_start(1, xsend.at[1], xbuf.at[1])
    arrive(sig_x)

    sre, sim = forward(xbuf[1])
    tre, tim = spec[0], spec[1]
    pre, pim = split(sre * tre - sim * tim), split(sre * tim + sim * tre)
    cos_p, sin_p = (inner[0], inner[1]), (inner[2], inner[3])
    re = dot3(pre, cos_p) - dot3(pim, sin_p)
    im = dot3(pim, cos_p) + dot3(pre, sin_p)
    cos_t, sin_t = tall(twist[0]), tall(twist[1])
    re, im = split(re * cos_t - im * sin_t), split(im * cos_t + re * sin_t)
    csend[...] = (dot3((back[0], back[1]), re) + dot3((back[2], back[3]), im)).astype(BF16)

    conv_x = x_start(2, csend, cbuf)
    arrive(conv_x)
    dsend[...] = dot(perm[1], cbuf[...]).astype(BF16)
    conv_z = z_start(2, dsend, conv)
    arrive(conv_z)

    gated = (
        gate[...].astype(F32) * (conv[...].astype(F32) + skip_cols[...] * sig[...])
    ).astype(BF16)

    reach = ny // 2
    offsets = [reach]
    for o in range(reach - 1, 0, -1):
        offsets += [o, -o]
    offsets += [0]
    slot = {o: n for n, o in enumerate(offsets)}
    slot[-reach] = 0

    def weight_rows(o, side):
        return w_t[pl.ds(pl.multiple_of((y_at(o) * 2 + side) * drows, drows), drows), :]

    pair = []
    for n, o in enumerate(offsets):
        psend[n] = dot(weight_rows(o, 1 - core), gated).astype(BF16)
        copy = pltpu.make_async_remote_copy(
            src_ref=psend.at[n],
            dst_ref=precv.at[n],
            send_sem=ps_sem.at[n],
            recv_sem=pr_sem.at[n],
            device_id=partner,
            device_id_type=MESH,
        )
        copy.start()
        pair.append(copy)
        own[n] = dot(weight_rows(o, core), gated)
    started.extend(pair)

    there = set()

    def chip_sum(o, lanes):
        n = slot[o]
        if n not in there:
            pair[n].wait_recv()
            there.add(n)
        return own[n, :, lanes] + precv[n, :, lanes].astype(F32)

    low, high = pl.ds(0, half), pl.ds(half, half)
    rings = [(1, low, reach), (-1, high, reach), (1, high, reach - 1), (-1, low, reach - 1)]
    last = [None] * len(rings)
    for step in range(reach):
        for r, (way, lanes, begin) in enumerate(rings):
            distance = begin - step
            if distance < 1:
                continue
            total = chip_sum(way * distance, lanes)
            if last[r] is not None:
                last[r].wait_recv()
                total = total + rrecv[r, step - 1].astype(F32)
            rsend[r, step] = total.astype(BF16)
            copy = pltpu.make_async_remote_copy(
                src_ref=rsend.at[r, step],
                dst_ref=rrecv.at[r, step],
                send_sem=rs_sem.at[r, step],
                recv_sem=rr_sem.at[r, step],
                device_id=y_peer(way),
                device_id_type=MESH,
            )
            copy.start()
            started.append(copy)
            last[r] = copy
    for lanes, ends in ((low, (0, 3)), (high, (1, 2))):
        total = chip_sum(0, lanes)
        for r in ends:
            if last[r] is not None:
                last[r].wait_recv()
                total = total + rrecv[r, rings[r][2] - 1].astype(F32)
        out[:, lanes] = total.astype(BF16)

    for copy in started:
        copy.wait_send()


def body(nz, nx, ny, gate_q, key_k, value_v, filter_taps, skip_bias, w_out):
    channels, width = key_k.shape
    depth = w_out.shape[1]
    drows = depth // (2 * ny)
    reach = ny // 2
    consts = tables(nz, nx, channels // (nz * nx), width)
    vmem = lambda *shape, dtype=BF16: pltpu.VMEM(shape, dtype)
    dma = lambda *shape: pltpu.SemaphoreType.DMA(shape)
    scratch = [
        vmem(channels, width, dtype=F32),
        vmem(channels, width, dtype=F32),
        vmem(depth, channels),
        vmem(2, channels, width),
        vmem(2, channels, width),
        vmem(2, channels, width),
        vmem(2, channels, width),
        vmem(2, channels, width, dtype=F32),
        vmem(channels, width),
        vmem(channels, width),
        vmem(channels, width),
        vmem(channels, width),
        vmem(ny, drows, width),
        vmem(ny, drows, width),
        vmem(ny, drows, width, dtype=F32),
        vmem(4, reach, drows, width // 2),
        vmem(4, reach, drows, width // 2),
        dma(3, nz - 1), dma(3, nz - 1),
        dma(3, nx - 1), dma(3, nx - 1),
        dma(ny), dma(ny),
        dma(4, reach), dma(4, reach),
    ]
    return pl.pallas_call(
        functools.partial(kernel, nz, nx, ny),
        out_shape=jax.ShapeDtypeStruct((drows, width), BF16),
        in_specs=[pl.BlockSpec(memory_space=pltpu.VMEM)] * 11,
        out_specs=pl.BlockSpec(memory_space=pltpu.VMEM),
        scratch_shapes=scratch,
        compiler_params=pltpu.CompilerParams(
            collective_id=0, has_side_effects=True, vmem_limit_bytes=40 << 20
        ),
    )(gate_q, key_k, value_v, filter_taps, skip_bias.reshape(1, channels), w_out, *consts)


def solution(mesh):
    nz, ny = mesh.shape["ctx"] // NX, mesh.shape["tp"] // 2
    return jax.shard_map(
        functools.partial(body, nz, NX, ny),
        mesh=mesh,
        in_specs=(
            P("tp", "ctx"),
            P("tp", "ctx"),
            P("tp", "ctx"),
            P("tp", "ctx"),
            P("tp"),
            P("tp", None),
        ),
        out_specs=P("tp", "ctx"),
        check_vma=False,
    )
```

time: 148 us -> 85.8 us (0.58)
  the two profiles are of different devices: /device:TPU:1 before, /device:TPU:2 now
where the time goes in v1:
time: 85.8 us; the launch traced here: 85.4 us
  Pallas kernels  73.8 us (86%)
  local copies, waits for them, and re-layouts  11.6 us (14%)
    pallas_call x1, Pallas kernels, body(): pl.pallas_call(functools.partial(kernel, nz, nx, ny), out_shape=jax.Shape...  73.8 us
    unnamed x23, local copies, waits for them, and re-layouts  11.6 us

profile of v1, /device:TPU:2, one launch (start us, length us, event | category | flops | bytes accessed | tf_op | source)
XLA Modules:
  0.0 85.4 jit_solution(5459713964722189373)
XLA Ops:
  0.0 0.0 copy-start
  0.0 1.6 %copy-done = bf16[256,4096]{1,0:T(8,128)(2,1)S(1)} copy-done((bf16[256,4096]{1,0:T(8,128)(2,1)S(1)}, bf16[256,4096]{1,0:T(8,128)(2,1)}, u32[]{:S(2)}) %copy-start) | copy-done | bytes 2097176
  1.6 0.0 copy-start.1
  1.6 1.0 %copy-done.1 = bf16[4,256,256]{2,1,0:T(8,128)(2,1)S(1)} copy-done((bf16[4,256,256]{2,1,0:T(8,128)(2,1)S(1)}, bf16[4,256,256]{2,1,0:T(8,128)(2,1)}, u32[]{:S(2)}) %copy-start.1) | copy-done | bytes 524312
  2.6 0.0 copy-start.2
  2.6 1.0 %copy-done.2 = bf16[4,256,256]{2,1,0:T(8,128)(2,1)S(1)} copy-done((bf16[4,256,256]{2,1,0:T(8,128)(2,1)S(1)}, bf16[4,256,256]{2,1,0:T(8,128)(2,1)}, u32[]{:S(2)}) %copy-start.2) | copy-done | bytes 524312
  3.7 0.0 copy-start.3
  3.7 1.0 %copy-done.3 = bf16[4,256,256]{2,1,0:T(8,128)(2,1)S(1)} copy-done((bf16[4,256,256]{2,1,0:T(8,128)(2,1)S(1)}, bf16[4,256,256]{2,1,0:T(8,128)(2,1)}, u32[]{:S(2)}) %copy-start.3) | copy-done | bytes 524312
  4.7 0.0 copy-start.4
  4.7 0.9 %copy-done.4 = f32[256,256]{1,0:T(8,128)S(1)} copy-done((f32[256,256]{1,0:T(8,128)S(1)}, f32[256,256]{1,0:T(8,128)}, u32[]{:S(2)}) %copy-start.4) | copy-done | bytes 262168
  5.7 0.0 copy-start.5
  5.7 0.9 %copy-done.5 = bf16[2,256,256]{2,1,0:T(8,128)(2,1)S(1)} copy-done((bf16[2,256,256]{2,1,0:T(8,128)(2,1)S(1)}, bf16[2,256,256]{2,1,0:T(8,128)(2,1)}, u32[]{:S(2)}) %copy-start.5) | copy-done | bytes 262168
  6.6 0.0 copy-start.6
  6.6 0.9 %copy-done.6 = bf16[256,256]{1,0:T(8,128)(2,1)S(1)} copy-done((bf16[256,256]{1,0:T(8,128)(2,1)S(1)}, bf16[256,256]{1,0:T(8,128)(2,1)}, u32[]{:S(2)}) %copy-start.6) | copy-done | bytes 131096
  7.5 0.0 copy-start.7
  7.5 0.9 %copy-done.7 = bf16[256,256]{1,0:T(8,128)(2,1)S(1)} copy-done((bf16[256,256]{1,0:T(8,128)(2,1)S(1)}, bf16[256,256]{1,0:T(8,128)(2,1)}, u32[]{:S(2)}) %copy-start.7) | copy-done | bytes 131096
  8.4 0.0 copy-start.8
  8.4 0.9 %copy-done.8 = bf16[256,256]{1,0:T(8,128)(2,1)S(1)} copy-done((bf16[256,256]{1,0:T(8,128)(2,1)S(1)}, bf16[256,256]{1,0:T(8,128)(2,1)}, u32[]{:S(2)}) %copy-start.8) | copy-done | bytes 131096
  9.3 0.0 copy-start.9
  9.3 0.9 %copy-done.9 = f32[2,64,256]{2,1,0:T(8,128)S(1)} copy-done((f32[2,64,256]{2,1,0:T(8,128)S(1)}, f32[2,64,256]{2,1,0:T(8,128)}, u32[]{:S(2)}) %copy-start.9) | copy-done | bytes 131096
  10.2 0.0 copy-start.10
  10.2 0.7 copy-done.10
  10.9 73.8 %shard_map.109 = bf16[256,256]{1,0:T(8,128)(2,1)S(1)} custom-call(bf16[256,256]{1,0:T(8,128)(2,1)S(1)} %copy-done.6, bf16[256,256]{1,0:T(8,128)(2,1)S(1)} %copy-done.7, bf16[256,256]{1,0:T(8,128)(2,1)S(1)} %copy-done.8, f32[256,256]{1,0:T(8,128)S(1)} %copy-done.4, f32[1,256]{1,0:T(1,128)S(1)} %bitcast.1, bf16[256,4096]{1,0:T(8,128)(2,1)S(1)} %copy-done, ...), custom_call_target="tpu_custom_call" | custom-call | tf_op jit(solution)/shard_map/pallas_call | solution.py:318
  84.7 0.7 copy.13
Async XLA Ops:
  0.0 1.6 %copy-start = (bf16[256,4096]{1,0:T(8,128)(2,1)S(1)}, bf16[256,4096]{1,0:T(8,128)(2,1)}, u32[]{:S(2)}) copy-start(bf16[256,4096]{1,0:T(8,128)(2,1)} %w.1) | copy-start | bytes 6291460
  1.6 1.0 %copy-start.1 = (bf16[4,256,256]{2,1,0:T(8,128)(2,1)S(1)}, bf16[4,256,256]{2,1,0:T(8,128)(2,1)}, u32[]{:S(2)}) copy-start(bf16[4,256,256]{2,1,0:T(8,128)(2,1)} %constant.13.clone.inner) | copy-start | bytes 1572868
  2.6 1.0 %copy-start.2 = (bf16[4,256,256]{2,1,0:T(8,128)(2,1)S(1)}, bf16[4,256,256]{2,1,0:T(8,128)(2,1)}, u32[]{:S(2)}) copy-start(bf16[4,256,256]{2,1,0:T(8,128)(2,1)} %constant.11.clone.back) | copy-start | bytes 1572868
  3.7 1.0 %copy-start.3 = (bf16[4,256,256]{2,1,0:T(8,128)(2,1)S(1)}, bf16[4,256,256]{2,1,0:T(8,128)(2,1)}, u32[]{:S(2)}) copy-start(bf16[4,256,256]{2,1,0:T(8,128)(2,1)} %constant.10.clone.ahead) | copy-start | bytes 1572868
  4.7 0.9 %copy-start.4 = (f32[256,256]{1,0:T(8,128)S(1)}, f32[256,256]{1,0:T(8,128)}, u32[]{:S(2)}) copy-start(f32[256,256]{1,0:T(8,128)} %taps.1) | copy-start | bytes 786436
  5.7 0.9 %copy-start.5 = (bf16[2,256,256]{2,1,0:T(8,128)(2,1)S(1)}, bf16[2,256,256]{2,1,0:T(8,128)(2,1)}, u32[]{:S(2)}) copy-start(bf16[2,256,256]{2,1,0:T(8,128)(2,1)} %constant.14.clone.perm) | copy-start | bytes 786436
  6.6 0.9 %copy-start.6 = (bf16[256,256]{1,0:T(8,128)(2,1)S(1)}, bf16[256,256]{1,0:T(8,128)(2,1)}, u32[]{:S(2)}) copy-start(bf16[256,256]{1,0:T(8,128)(2,1)} %gate.1) | copy-start | bytes 393220
  7.5 0.9 %copy-start.7 = (bf16[256,256]{1,0:T(8,128)(2,1)S(1)}, bf16[256,256]{1,0:T(8,128)(2,1)}, u32[]{:S(2)}) copy-start(bf16[256,256]{1,0:T(8,128)(2,1)} %key.1) | copy-start | bytes 393220
  8.4 0.9 %copy-start.8 = (bf16[256,256]{1,0:T(8,128)(2,1)S(1)}, bf16[256,256]{1,0:T(8,128)(2,1)}, u32[]{:S(2)}) copy-start(bf16[256,256]{1,0:T(8,128)(2,1)} %value.1) | copy-start | bytes 393220
  9.3 0.9 %copy-start.9 = (f32[2,64,256]{2,1,0:T(8,128)S(1)}, f32[2,64,256]{2,1,0:T(8,128)}, u32[]{:S(2)}) copy-start(f32[2,64,256]{2,1,0:T(8,128)} %constant.12.clone.twist) | copy-start | bytes 393220
  10.2 0.7 copy-start.10

commit v2 on v1

--- a/solution.py
+++ b/solution.py
@@ -60,8 +60,9 @@
 
 def kernel(
     nz, nx, ny,
-    gate, key, value, taps, skip, w, ahead, back, twist, inner, perm,
+    gate_h, key_h, value_h, taps_h, skip_h, w_h, ahead_h, back_h, twist_h, inner_h, perm_h,
     out,
+    gate, key, value, taps, skip, w, ahead, back, twist, inner, perm, in_sem,
     sig, skip_cols, w_t, zsend, zbuf, xsend, xbuf, spec, csend, cbuf, dsend, conv,
     psend, precv, own, rsend, rrecv,
     zs_sem, zr_sem, xs_sem, xr_sem, ps_sem, pr_sem, rs_sem, rr_sem,
@@ -102,6 +103,27 @@
         z_order += [o, -o]
     x_order = list(range(1, nx))
 
+    loads = {}
+    for n, (name, source, target) in enumerate((
+        ("taps", taps_h, taps),
+        ("key", key_h, key),
+        ("value", value_h, value),
+        ("perm", perm_h, perm),
+        ("w", w_h, w),
+        ("skip", skip_h, skip),
+        ("ahead", ahead_h, ahead),
+        ("twist", twist_h, twist),
+        ("inner", inner_h, inner),
+        ("back", back_h, back),
+        ("gate", gate_h, gate),
+    )):
+        loads[name] = pltpu.make_async_copy(source, target, in_sem.at[n])
+        loads[name].start()
+
+    def loaded(*names):
+        for name in names:
+            loads[name].wait()
+
     barrier = pltpu.get_barrier_semaphore()
     peers = [z_peer(o) for o in z_order] + [x_peer(o) for o in x_order]
     peers += [partner, y_peer(1), y_peer(-1)]
@@ -136,13 +158,19 @@
             device_id_type=MESH,
         )
 
-    def z_start(kind, source, target):
+    far = len(z_order) // 2
+
+    def z_copies(kind, source, target):
         copies = [z_copy(kind, source, target, n, o) for n, o in enumerate(z_order)]
+        started.extend(copies)
+        return copies
+
+    def z_start(copies):
         for copy in copies:
             copy.start()
+
+    def z_keep(source, target):
         target[rows_z(z), :] = source[rows_z(z), :]
-        started.extend(copies)
-        return copies
 
     def x_start(kind, source, target):
         copies = [x_copy(kind, source, target, n, o) for n, o in enumerate(x_order)]
@@ -169,27 +197,38 @@
             dot3(mid_im, cos_p) - dot3(mid_re, sin_p),
         )
 
+    loaded("taps")
     zsend[0] = taps[...].astype(BF16)
-    pl.semaphore_wait(barrier, len(peers))
-    taps_z = z_start(0, zsend.at[0], zbuf.at[0])
+    loaded("key", "value")
     sig[...] = key[...].astype(F32) * value[...].astype(F32)
     zsend[1] = sig[...].astype(BF16)
-    sig_z = z_start(1, zsend.at[1], zbuf.at[1])
-
+    taps_z = z_copies(0, zsend.at[0], zbuf.at[0])
+    sig_z = z_copies(1, zsend.at[1], zbuf.at[1])
+    pl.semaphore_wait(barrier, len(peers))
+    z_start(taps_z[:far])
+    z_start(sig_z[:far])
+    z_start(taps_z[far:])
+    z_start(sig_z[far:])
+    z_keep(zsend.at[0], zbuf.at[0])
+    z_keep(zsend.at[1], zbuf.at[1])
+
+    loaded("skip", "w")
     skip_cols[...] = jnp.broadcast_to(skip[...], (width, channels)).T
     for j in range(w.shape[1] // drows):
         w_t[pl.ds(j * drows, drows), :] = w[:, pl.ds(j * drows, drows)].T
 
+    loaded("perm")
     arrive(taps_z)
     xsend[0] = dot(perm[0], zbuf[0]).astype(BF16)
     taps_x = x_start(0, xsend.at[0], xbuf.at[0])
+    arrive(sig_z)
+    xsend[1] = dot(perm[0], zbuf[1]).astype(BF16)
+    sig_x = x_start(1, xsend.at[1], xbuf.at[1])
+    loaded("ahead", "twist", "inner")
     arrive(taps_x)
     spec_re, spec_im = forward(xbuf[0])
     spec[0] = spec_re
     spec[1] = spec_im
-    arrive(sig_z)
-    xsend[1] = dot(perm[0], zbuf[1]).astype(BF16)
-    sig_x = x_start(1, xsend.at[1], xbuf.at[1])
     arrive(sig_x)
 
     sre, sim = forward(xbuf[1])
@@ -200,12 +239,16 @@
     im = dot3(pim, cos_p) + dot3(pre, sin_p)
     cos_t, sin_t = tall(twist[0]), tall(twist[1])
     re, im = split(re * cos_t - im * sin_t), split(im * cos_t + re * sin_t)
+    loaded("back")
     csend[...] = (dot3((back[0], back[1]), re) + dot3((back[2], back[3]), im)).astype(BF16)
 
     conv_x = x_start(2, csend, cbuf)
     arrive(conv_x)
     dsend[...] = dot(perm[1], cbuf[...]).astype(BF16)
-    conv_z = z_start(2, dsend, conv)
+    conv_z = z_copies(2, dsend, conv)
+    z_start(conv_z)
+    z_keep(dsend, conv)
+    loaded("gate")
     arrive(conv_z)
 
     gated = (
@@ -292,7 +335,12 @@
     consts = tables(nz, nx, channels // (nz * nx), width)
     vmem = lambda *shape, dtype=BF16: pltpu.VMEM(shape, dtype)
     dma = lambda *shape: pltpu.SemaphoreType.DMA(shape)
-    scratch = [
+    operands = (
+        gate_q, key_k, value_v, filter_taps, skip_bias.reshape(1, channels), w_out, *consts
+    )
+    scratch = [vmem(*a.shape, dtype=a.dtype) for a in operands]
+    scratch += [
+        dma(len(operands)),
         vmem(channels, width, dtype=F32),
         vmem(channels, width, dtype=F32),
         vmem(depth, channels),
@@ -318,13 +366,13 @@
     return pl.pallas_call(
         functools.partial(kernel, nz, nx, ny),
         out_shape=jax.ShapeDtypeStruct((drows, width), BF16),
-        in_specs=[pl.BlockSpec(memory_space=pltpu.VMEM)] * 11,
+        in_specs=[pl.BlockSpec(memory_space=pltpu.HBM)] * len(operands),
         out_specs=pl.BlockSpec(memory_space=pltpu.VMEM),
         scratch_shapes=scratch,
         compiler_params=pltpu.CompilerParams(
-            collective_id=0, has_side_effects=True, vmem_limit_bytes=40 << 20
+            collective_id=0, has_side_effects=True, vmem_limit_bytes=60 << 20
         ),
-    )(gate_q, key_k, value_v, filter_taps, skip_bias.reshape(1, channels), w_out, *consts)
+    )(*operands)
 
 
 def solution(mesh):

time: 85.8 us -> 75.9 us (0.88)
  the two profiles are of different devices: /device:TPU:2 before, /device:TPU:1 now
where the time goes in v2:
time: 75.9 us; the launch traced here: 74.5 us
  Pallas kernels  72.9 us (96%)
  local copies, waits for them, and re-layouts  1.57 us (2%)
    pallas_call x1, Pallas kernels, body(): pl.pallas_call(functools.partial(kernel, nz, nx, ny), out_shape=jax.Shape...  72.9 us
    unnamed x1, local copies, waits for them, and re-layouts  1.57 us

profile of v2, /device:TPU:1, one launch (start us, length us, event | category | flops | bytes accessed | tf_op | source)
XLA Modules:
  0.0 74.5 jit_solution(18004116986758417319)
XLA Ops:
  0.0 72.9 %shard_map.109 = bf16[256,256]{1,0:T(8,128)(2,1)} custom-call(bf16[256,256]{1,0:T(8,128)(2,1)} %gate_h.1, bf16[256,256]{1,0:T(8,128)(2,1)} %key_h.1, bf16[256,256]{1,0:T(8,128)(2,1)} %value_h.1, f32[256,256]{1,0:T(8,128)} %taps_h.1, f32[1,256]{1,0:T(1,128)} %bitcast.1, bf16[256,4096]{1,0:T(8,128)(2,1)} %w_h.1, bf16[4,256,256]{2,1,0:T(8,128)(2,1)} %constant.10.clone.ahead_h, ...), custom_call_target="tpu_custom_call" | custom-call | tf_op jit(solution)/shard_map/pallas_call | solution.py:366
  72.9 1.6 %copy.13 = bf16[256,256]{1,0:T(8,128)(2,1)} copy(bf16[256,256]{1,0:T(8,128)(2,1)} %shard_map.109) | data formatting | bytes 262144

commit v3 on v2

--- a/solution.py
+++ b/solution.py
@@ -12,6 +12,7 @@
 MESH = pl.DeviceIdType.MESH
 F32 = jnp.float32
 BF16 = jnp.bfloat16
+ROW_PARTS = 2
 NX = 4
 
 
@@ -103,6 +104,12 @@
         z_order += [o, -o]
     x_order = list(range(1, nx))
 
+    barrier = pltpu.get_barrier_semaphore()
+    peers = [z_peer(o) for o in z_order] + [x_peer(o) for o in x_order]
+    peers += [partner, y_peer(1), y_peer(-1)]
+    for peer in peers:
+        pl.semaphore_signal(barrier, inc=1, device_id=peer, device_id_type=MESH)
+
     loads = {}
     for n, (name, source, target) in enumerate((
         ("taps", taps_h, taps),
@@ -124,12 +131,6 @@
         for name in names:
             loads[name].wait()
 
-    barrier = pltpu.get_barrier_semaphore()
-    peers = [z_peer(o) for o in z_order] + [x_peer(o) for o in x_order]
-    peers += [partner, y_peer(1), y_peer(-1)]
-    for peer in peers:
-        pl.semaphore_signal(barrier, inc=1, device_id=peer, device_id_type=MESH)
-
     started = []
 
     def rows_z(i):
@@ -266,10 +267,11 @@
     def weight_rows(o, side):
         return w_t[pl.ds(pl.multiple_of((y_at(o) * 2 + side) * drows, drows), drows), :]
 
-    pair = []
-    for n, o in enumerate(offsets):
-        psend[n] = dot(weight_rows(o, 1 - core), gated).astype(BF16)
-        copy = pltpu.make_async_remote_copy(
+    pair = {}
+
+    def send_pair(n):
+        psend[n] = dot(weight_rows(offsets[n], 1 - core), gated).astype(BF16)
+        pair[n] = pltpu.make_async_remote_copy(
             src_ref=psend.at[n],
             dst_ref=precv.at[n],
             send_sem=ps_sem.at[n],
@@ -277,29 +279,37 @@
             device_id=partner,
             device_id_type=MESH,
         )
-        copy.start()
-        pair.append(copy)
-        own[n] = dot(weight_rows(o, core), gated)
-    started.extend(pair)
+        pair[n].start()
+        started.append(pair[n])
+
+    def keep_own(n):
+        own[n] = dot(weight_rows(offsets[n], core), gated)
 
     there = set()
 
-    def chip_sum(o, lanes):
+    def chip_sum(o, rows, lanes):
         n = slot[o]
         if n not in there:
             pair[n].wait_recv()
             there.add(n)
-        return own[n, :, lanes] + precv[n, :, lanes].astype(F32)
+        return own[n, rows, lanes] + precv[n, rows, lanes].astype(F32)
 
     low, high = pl.ds(0, half), pl.ds(half, half)
-    rings = [(1, low, reach), (-1, high, reach), (1, high, reach - 1), (-1, low, reach - 1)]
+    parts = drows // ROW_PARTS
+    pieces = [pl.ds(k * parts, parts) for k in range(ROW_PARTS)]
+    rings = []
+    for begin in (reach, reach - 1):
+        for rows in pieces:
+            rings += [(1, rows, low if begin == reach else high, begin)]
+            rings += [(-1, rows, high if begin == reach else low, begin)]
     last = [None] * len(rings)
-    for step in range(reach):
-        for r, (way, lanes, begin) in enumerate(rings):
+
+    def ring_step(step):
+        for r, (way, rows, lanes, begin) in enumerate(rings):
             distance = begin - step
             if distance < 1:
                 continue
-            total = chip_sum(way * distance, lanes)
+            total = chip_sum(way * distance, rows, lanes)
             if last[r] is not None:
                 last[r].wait_recv()
                 total = total + rrecv[r, step - 1].astype(F32)
@@ -315,13 +325,21 @@
             copy.start()
             started.append(copy)
             last[r] = copy
-    for lanes, ends in ((low, (0, 3)), (high, (1, 2))):
-        total = chip_sum(0, lanes)
-        for r in ends:
-            if last[r] is not None:
-                last[r].wait_recv()
-                total = total + rrecv[r, rings[r][2] - 1].astype(F32)
-        out[:, lanes] = total.astype(BF16)
+
+    for n in range(ny):
+        send_pair(n)
+    for n in range(ny):
+        keep_own(n)
+    for step in range(reach):
+        ring_step(step)
+    for rows in pieces:
+        for lanes in (low, high):
+            total = chip_sum(0, rows, lanes)
+            for r, ring in enumerate(rings):
+                if ring[1] is rows and ring[2] is lanes and last[r] is not None:
+                    last[r].wait_recv()
+                    total = total + rrecv[r, ring[3] - 1].astype(F32)
+            out[rows, lanes] = total.astype(BF16)
 
     for copy in started:
         copy.wait_send()
@@ -356,12 +374,12 @@
         vmem(ny, drows, width),
         vmem(ny, drows, width),
         vmem(ny, drows, width, dtype=F32),
-        vmem(4, reach, drows, width // 2),
-        vmem(4, reach, drows, width // 2),
+        vmem(4 * ROW_PARTS, reach, drows // ROW_PARTS, width // 2),
+        vmem(4 * ROW_PARTS, reach, drows // ROW_PARTS, width // 2),
         dma(3, nz - 1), dma(3, nz - 1),
         dma(3, nx - 1), dma(3, nx - 1),
         dma(ny), dma(ny),
-        dma(4, reach), dma(4, reach),
+        dma(4 * ROW_PARTS, reach), dma(4 * ROW_PARTS, reach),
     ]
     return pl.pallas_call(
         functools.partial(kernel, nz, nx, ny),
@@ -370,9 +388,9 @@
         out_specs=pl.BlockSpec(memory_space=pltpu.VMEM),
         scratch_shapes=scratch,
         compiler_params=pltpu.CompilerParams(
-            collective_id=0, has_side_effects=True, vmem_limit_bytes=60 << 20
+            collective_id=0, has_side_effects=True, vmem_limit_bytes=40 << 20
         ),
-    )(*operands)
+    )(*[pltpu.with_memory_space_constraint(a, pltpu.HBM) for a in operands])
 
 
 def solution(mesh):

time: 75.9 us -> 73.7 us (0.971)
  local copies, waits for them, and re-layouts: 1.57 us -> 0.66 us
  Pallas kernels: 72.9 us -> 72 us
    pallas_call x1, Pallas kernels: 72.9 us -> 72 us  [body(): pl.pallas_call(functools.partial(kernel, nz, nx, ny), out_shape=jax.Shape...]
    unnamed x1, local copies, waits for them, and re-layouts: 1.57 us -> 0.66 us
where the time goes in v3:
time: 73.7 us; the launch traced here: 72.6 us
  Pallas kernels  72 us (98%)
    pallas_call x1, Pallas kernels, body(): pl.pallas_call(functools.partial(kernel, nz, nx, ny), out_shape=jax.Shape...  72 us

profile of v3, /device:TPU:1, one launch (start us, length us, event | category | flops | bytes accessed | tf_op | source)
XLA Modules:
  0.0 72.6 jit_solution(418069070301516536)
XLA Ops:
  0.0 72.0 %shard_map.109 = bf16[256,256]{1,0:T(8,128)(2,1)S(1)} custom-call(bf16[256,256]{1,0:T(8,128)(2,1)} %gate_h.1, bf16[256,256]{1,0:T(8,128)(2,1)} %key_h.1, bf16[256,256]{1,0:T(8,128)(2,1)} %value_h.1, f32[256,256]{1,0:T(8,128)} %taps_h.1, f32[1,256]{1,0:T(1,128)} %bitcast.1, bf16[256,4096]{1,0:T(8,128)(2,1)} %w_h.1, ...), custom_call_target="tpu_custom_call" | custom-call | tf_op jit(solution)/shard_map/pallas_call | solution.py:384
  72.0 0.7 copy.13

commit v4 on v3

--- a/solution.py
+++ b/solution.py
@@ -12,7 +12,8 @@
 MESH = pl.DeviceIdType.MESH
 F32 = jnp.float32
 BF16 = jnp.bfloat16
-ROW_PARTS = 2
+ROW_PARTS = 4
+OFFSETS = (4, 3, -3, 2, -2, 1, -1, 0)
 NX = 4
 
 
@@ -106,7 +107,7 @@
 
     barrier = pltpu.get_barrier_semaphore()
     peers = [z_peer(o) for o in z_order] + [x_peer(o) for o in x_order]
-    peers += [partner, y_peer(1), y_peer(-1)]
+    peers += [partner, y_peer(1), y_peer(-1), y_peer(2), y_peer(-2)]
     for peer in peers:
         pl.semaphore_signal(barrier, inc=1, device_id=peer, device_id_type=MESH)
 
@@ -256,13 +257,8 @@
         gate[...].astype(F32) * (conv[...].astype(F32) + skip_cols[...] * sig[...])
     ).astype(BF16)
 
-    reach = ny // 2
-    offsets = [reach]
-    for o in range(reach - 1, 0, -1):
-        offsets += [o, -o]
-    offsets += [0]
-    slot = {o: n for n, o in enumerate(offsets)}
-    slot[-reach] = 0
+    slot = {o: n for n, o in enumerate(OFFSETS)}
+    slot[-4] = slot[4]
 
     def weight_rows(o, side):
         return w_t[pl.ds(pl.multiple_of((y_at(o) * 2 + side) * drows, drows), drows), :]
@@ -270,7 +266,7 @@
     pair = {}
 
     def send_pair(n):
-        psend[n] = dot(weight_rows(offsets[n], 1 - core), gated).astype(BF16)
+        psend[n] = dot(weight_rows(OFFSETS[n], 1 - core), gated).astype(BF16)
         pair[n] = pltpu.make_async_remote_copy(
             src_ref=psend.at[n],
             dst_ref=precv.at[n],
@@ -283,7 +279,7 @@
         started.append(pair[n])
 
     def keep_own(n):
-        own[n] = dot(weight_rows(offsets[n], core), gated)
+        own[n] = dot(weight_rows(OFFSETS[n], core), gated)
 
     there = set()
 
@@ -294,52 +290,62 @@
             there.add(n)
         return own[n, rows, lanes] + precv[n, rows, lanes].astype(F32)
 
-    low, high = pl.ds(0, half), pl.ds(half, half)
+    low, high, every = pl.ds(0, half), pl.ds(half, half), pl.ds(0, width)
+    ways = ((0, 1, low), (1, -1, high))
     parts = drows // ROW_PARTS
-    pieces = [pl.ds(k * parts, parts) for k in range(ROW_PARTS)]
-    rings = []
-    for begin in (reach, reach - 1):
-        for rows in pieces:
-            rings += [(1, rows, low if begin == reach else high, begin)]
-            rings += [(-1, rows, high if begin == reach else low, begin)]
-    last = [None] * len(rings)
-
-    def ring_step(step):
-        for r, (way, rows, lanes, begin) in enumerate(rings):
-            distance = begin - step
-            if distance < 1:
-                continue
-            total = chip_sum(way * distance, rows, lanes)
-            if last[r] is not None:
-                last[r].wait_recv()
-                total = total + rrecv[r, step - 1].astype(F32)
-            rsend[r, step] = total.astype(BF16)
-            copy = pltpu.make_async_remote_copy(
-                src_ref=rsend.at[r, step],
-                dst_ref=rrecv.at[r, step],
-                send_sem=rs_sem.at[r, step],
-                recv_sem=rr_sem.at[r, step],
-                device_id=y_peer(way),
-                device_id_type=MESH,
-            )
-            copy.start()
-            started.append(copy)
-            last[r] = copy
-
-    for n in range(ny):
+    pieces = [(k, pl.ds(k * parts, parts)) for k in range(ROW_PARTS)]
+    hops = {}
+
+    def hop(way, role, piece, lanes, target):
+        k, rows = piece
+        copy = pltpu.make_async_remote_copy(
+            src_ref=rsend.at[way, role, rows, lanes],
+            dst_ref=rrecv.at[way, role, rows, lanes],
+            send_sem=rs_sem.at[way, role, k],
+            recv_sem=rr_sem.at[way, role, k],
+            device_id=y_peer(target),
+            device_id_type=MESH,
+        )
+        copy.start()
+        started.append(copy)
+        hops[way, role, k] = copy
+
+    def came(way, role, piece, lanes):
+        return rrecv[way, role, piece[1], lanes].astype(F32)
+
+    for n in range(8):
         send_pair(n)
-    for n in range(ny):
+    for n in range(8):
         keep_own(n)
-    for step in range(reach):
-        ring_step(step)
-    for rows in pieces:
-        for lanes in (low, high):
-            total = chip_sum(0, rows, lanes)
-            for r, ring in enumerate(rings):
-                if ring[1] is rows and ring[2] is lanes and last[r] is not None:
-                    last[r].wait_recv()
-                    total = total + rrecv[r, ring[3] - 1].astype(F32)
-            out[rows, lanes] = total.astype(BF16)
+    for piece in pieces:
+        for way, sign, lanes in ways:
+            rsend[way, 3, piece[1], lanes] = chip_sum(4 * sign, piece[1], lanes).astype(BF16)
+            hop(way, 3, piece, lanes, 2 * sign)
+        for way, sign, _ in ways:
+            rsend[way, 2, piece[1], :] = chip_sum(3 * sign, piece[1], every).astype(BF16)
+            hop(way, 2, piece, every, sign)
+    for piece in pieces:
+        for way, sign, extra in ways:
+            hops[way, 3, piece[0]].wait_recv()
+            hops[way, 2, piece[0]].wait_recv()
+            for lanes in (low, high):
+                total = chip_sum(2 * sign, piece[1], lanes) + came(way, 2, piece, lanes)
+                if lanes is extra:
+                    total = total + came(way, 3, piece, lanes)
+                rsend[way, 1, piece[1], lanes] = total.astype(BF16)
+            hop(way, 1, piece, every, sign)
+    for piece in pieces:
+        for way, sign, _ in ways:
+            hops[way, 1, piece[0]].wait_recv()
+            total = chip_sum(sign, piece[1], every) + came(way, 1, piece, every)
+            rsend[way, 0, piece[1], :] = total.astype(BF16)
+            hop(way, 0, piece, every, sign)
+    for piece in pieces:
+        total = chip_sum(0, piece[1], every)
+        for way in (0, 1):
+            hops[way, 0, piece[0]].wait_recv()
+            total = total + came(way, 0, piece, every)
+        out[piece[1], :] = total.astype(BF16)
 
     for copy in started:
         copy.wait_send()
@@ -349,7 +355,6 @@
     channels, width = key_k.shape
     depth = w_out.shape[1]
     drows = depth // (2 * ny)
-    reach = ny // 2
     consts = tables(nz, nx, channels // (nz * nx), width)
     vmem = lambda *shape, dtype=BF16: pltpu.VMEM(shape, dtype)
     dma = lambda *shape: pltpu.SemaphoreType.DMA(shape)
@@ -374,12 +379,12 @@
         vmem(ny, drows, width),
         vmem(ny, drows, width),
         vmem(ny, drows, width, dtype=F32),
-        vmem(4 * ROW_PARTS, reach, drows // ROW_PARTS, width // 2),
-        vmem(4 * ROW_PARTS, reach, drows // ROW_PARTS, width // 2),
+        vmem(2, 4, drows, width),
+        vmem(2, 4, drows, width),
         dma(3, nz - 1), dma(3, nz - 1),
         dma(3, nx - 1), dma(3, nx - 1),
         dma(ny), dma(ny),
-        dma(4 * ROW_PARTS, reach), dma(4 * ROW_PARTS, reach),
+        dma(2, 4, ROW_PARTS), dma(2, 4, ROW_PARTS),
     ]
     return pl.pallas_call(
         functools.partial(kernel, nz, nx, ny),

time: 73.7 us -> 74.9 us (1.016)
  the two profiles are of different devices: /device:TPU:1 before, /device:TPU:8 now
where the time goes in v4:
time: 74.9 us; the launch traced here: 74.7 us
  Pallas kernels  74.1 us (99%)
    pallas_call x1, Pallas kernels, body(): pl.pallas_call(functools.partial(kernel, nz, nx, ny), out_shape=jax.Shape...  74.1 us

profile of v4, /device:TPU:8, one launch (start us, length us, event | category | flops | bytes accessed | tf_op | source)
XLA Modules:
  0.0 74.7 jit_solution(6207346165480373401)
XLA Ops:
  0.0 74.1 %shard_map.109 = bf16[256,256]{1,0:T(8,128)(2,1)S(1)} custom-call(bf16[256,256]{1,0:T(8,128)(2,1)} %gate_h.1, bf16[256,256]{1,0:T(8,128)(2,1)} %key_h.1, bf16[256,256]{1,0:T(8,128)(2,1)} %value_h.1, f32[256,256]{1,0:T(8,128)} %taps_h.1, f32[1,256]{1,0:T(1,128)} %bitcast.1, bf16[256,4096]{1,0:T(8,128)(2,1)} %w_h.1, ...), custom_call_target="tpu_custom_call" | custom-call | tf_op jit(solution)/shard_map/pallas_call | solution.py:389
  74.1 0.7 copy.13
